TPU v7x, 32 devices: a whole 2x2x4 slice. The times are simulated.
32 devices in a mesh: acq: 4 (over z), line: 8 (over y, x, core).
Axes of the slice: x: 2, y: 2, z: 4, core: 2. Of those that a mesh axis runs over, the one named last changes fastest.
Arguments:
- slc_stack: float32 [2, 64, 64, 512], P(None, 'acq', 'line'), may hold values from -6 to 6
- wavenumbers: float32 [64], replicated, may hold values from -0.8 to 0.8
Outputs:
- spectrum: bfloat16 [256, 64, 512], P(None, 'line', 'acq')
All inputs are finite; a program needn't handle non-finite values.
Results may differ from a plain program's by a relative error of at most 0.001.
Values sent between devices are 32-bit elements; how exact they have to be, the bound alone decides.
A program may use at most 64 MiB of HBM per device.

v0:
```python
import jax
import jax.numpy as jnp
from jax import lax
from jax.sharding import PartitionSpec as P

HEIGHTS = 256
epsilon = 1e-06


def with_line_halo(x, width):
    size, length = (lax.axis_size("line"), x.shape[2])
    up = [(i, i + 1) for i in range(size - 1)]
    down = [(j, i) for i, j in up]
    before = lax.ppermute(x[:, :, length - width :], "line", up)
    after = lax.ppermute(x[:, :, :width], "line", down)
    return jnp.concatenate([before, x, after], axis=2)


def range_halo(x, width):
    parts, acqs, lines, cells = x.shape
    size = lax.axis_size("acq")
    block = cells // size
    padded = jnp.pad(x, ((0, 0), (0, 0), (0, 0), (width, width)))
    edges = []
    for d in range(size):
        left = padded[..., d * block : d * block + width]
        start = (d + 1) * block + width
        right = padded[..., start : start + width]
        edges.append(jnp.concatenate([left, right], axis=3))
    sent = jnp.stack(edges).reshape(size, parts * acqs, lines * 2 * width)
    got = lax.all_to_all(sent, "acq", split_axis=0, concat_axis=0, tiled=True)
    got = got.reshape(size, parts, acqs, lines, 2 * width).transpose(1, 0, 2, 3, 4)
    return got.reshape(parts, size * acqs, lines, 2 * width)


def steering(wavenumbers, count):
    heights = jnp.arange(count, dtype=jnp.int32).astype(jnp.float32) - jnp.float32(count // 2)
    phases = wavenumbers[:, None] * heights[None, :]
    cosine_part = jnp.cos(phases).T
    sine_part = jnp.sin(phases).T
    upper = jnp.concatenate([cosine_part, sine_part], axis=1)
    lower = jnp.concatenate([-sine_part, cosine_part], axis=1)
    return jnp.concatenate([upper, lower], axis=0)


def beamform(stack_block, matrix, count):
    channels = stack_block.shape[0] * stack_block.shape[1]
    flat = stack_block.reshape(channels, -1)
    beams = jnp.dot(matrix, flat, precision=lax.Precision.HIGH, preferred_element_type=jnp.float32)
    beam_power = beams[:count] * beams[:count] + beams[count:] * beams[count:]
    energy = jnp.sum(flat * flat, axis=0)
    shape = stack_block.shape[2:]
    return (beam_power.reshape((count,) + shape), energy.reshape((1,) + shape))


def sum_range(field, count):
    total = field[..., 0:count]
    for offset in range(1, 7):
        total = total + field[..., offset : offset + count]
    return total


def sum_lines(field, count):
    total = field[..., 0:count, :]
    for offset in range(1, 7):
        total = total + field[..., offset : offset + count, :]
    return total


def body(slc_stack, wavenumbers):
    width = 3
    line_count = slc_stack.shape[2]
    tall = with_line_halo(slc_stack, width)
    edge = range_halo(tall, width)
    regrouped = lax.all_to_all(tall, "acq", split_axis=3, concat_axis=1, tiled=True)
    range_count = regrouped.shape[3]
    matrix = steering(wavenumbers, HEIGHTS)
    inner = beamform(regrouped, matrix, HEIGHTS)
    outer = beamform(edge, matrix, HEIGHTS)
    boxes = []
    for mid, rim in zip(inner, outer):
        mid, rim = (sum_lines(mid, line_count), sum_lines(rim, line_count))
        wide = jnp.concatenate([rim[..., :width], mid, rim[..., width:]], axis=-1)
        boxes.append(sum_range(wide, range_count))
    return (boxes[0] / (boxes[1] + epsilon)).astype(jnp.bfloat16)


def solution(mesh):
    placed = (P(None, "acq", "line", None), P())
    return jax.shard_map(
        body, mesh=mesh, in_specs=placed, out_specs=P(None, "line", "acq"), check_vma=False
    )
```

profile of v0, /device:TPU:0, one launch (start us, length us, event | category | flops | bytes accessed | tf_op | source)
XLA Modules:
  0.0 129.8 jit_solution(5151484903050266016)
XLA Ops:
  0.0 1.4 %fusion.34 = (f32[2,16,3,512]{3,2,1,0:T(4,128)S(1)}, f32[2,16,3,512]{3,2,1,0:T(4,128)S(1)}) fusion(f32[2,16,8,512]{3,2,1,0:T(8,128)} %param.2), kind=kLoop, calls=%fused_computation.87 | loop fusion | bytes 786432 | tf_op jit(solution)/shard_map/slice | solution.py:14
  1.5 2.4 %collective-permute-start = (f32[2,16,3,512]{3,1,2,0:T(8,128)S(1)}, f32[2,16,3,512]{3,1,2,0:T(8,128)S(1)}, u32[]{:S(2)}, u32[]{:S(2)}) collective-permute-start(f32[2,16,3,512]{3,1,2,0:T(8,128)S(1)} %copy.95), channel_id=1, source_target_pairs={{0,1},{1,2},{2,3},{3,4},{4,5},{5,6},{6,7},{8,9},{9,10},{10,11},{11... | collective-permute-start | bytes 589832 | tf_op jit(solution)/shard_map/ppermute | solution.py:14
  4.0 1.3 collective-permute-start.1
  5.3 8.2 %copy.75 = f32[2,16,8,512]{2,1,0,3:T(8,128)} copy(f32[2,16,8,512]{3,2,1,0:T(8,128)} %param.2) | data formatting | bytes 1048576 | tf_op args[0]
  13.5 0.5 multiply_sine_fusion
  14.1 7.5 %copy.74 = f32[2,16,3,512]{2,1,0,3:T(8,128)} copy(f32[2,16,3,512]{3,1,2,0:T(8,128)S(1)} %collective-permute-done) | data formatting | bytes 393216 | tf_op jit(solution)/shard_map/ppermute | solution.py:14
  21.6 7.5 %copy.76 = f32[2,16,3,512]{2,1,0,3:T(8,128)} copy(f32[2,16,3,512]{3,1,2,0:T(8,128)S(1)} %collective-permute-done.1) | data formatting | bytes 393216 | tf_op jit(solution)/shard_map/ppermute | solution.py:15
  29.1 10.5 %pad_maximum_fusion = f32[2,16,14,512]{2,1,0,3:T(8,128)S(1)} fusion(f32[2,16,3,512]{2,1,0,3:T(8,128)} %copy.76, f32[2,16,8,512]{2,1,0,3:T(8,128)} %copy.75, f32[2,16,3,512]{2,1,0,3:T(8,128)} %copy.74), kind=kLoop, calls=%fused_computation | loop fusion | flops 458752 | bytes 1835008 | tf_op jit(solution)/shard_map/concatenate | solution.py:16
  39.6 0.2 copy.78
  39.8 0.1 stack.16
  39.9 0.1 copy.82
  40.0 0.2 copy.79
  40.2 0.1 stack.17
  40.3 0.1 copy.97
  40.5 0.1 stack.15
  40.6 0.1 copy.81
  40.7 0.1 copy.98
  40.8 0.1 stack.18
  40.9 0.1 copy.84
  41.0 0.6 pad_maximum_fusion.5
  41.7 5.7 %all-to-all-start = ((f32[4,32,84]{2,1,0:T(8,128)}), f32[4,32,84]{2,1,0:T(8,128)S(1)}, u32[]{:S(2)}, u32[]{:S(2)}) async-start(f32[4,32,84]{2,1,0:T(8,128)} %pad_maximum_fusion.5), calls=%async_computation | async-start | bytes 131072 | tf_op jit(solution)/shard_map/all_to_all | solution.py:31
  47.4 13.2 %fusion.38 = f32[512,2,16,14]{3,2,1,0:T(8,128)} fusion(f32[2,16,3,512]{2,1,0,3:T(8,128)} %copy.76, f32[2,16,8,512]{2,1,0,3:T(8,128)} %copy.75, f32[2,16,3,512]{2,1,0,3:T(8,128)} %copy.74), kind=kLoop, calls=%fused_computation.90 | loop fusion | flops 458752 | bytes 1835008
  60.6 10.1 %reshape.44 = f32[4,1,57344]{2,1,0:T(1,128)} reshape(f32[512,2,16,14]{3,2,1,0:T(8,128)} %fusion.38) | data formatting | bytes 1835008
  70.7 5.1 %all-to-all-start.1 = ((f32[4,1,57344]{2,1,0:T(1,128)}), f32[4,1,57344]{2,1,0:T(1,128)S(1)}, u32[]{:S(2)}, u32[]{:S(2)}) async-start(f32[4,1,57344]{2,1,0:T(1,128)} %reshape.44), calls=%async_computation.1 | async-start | bytes 1835008 | tf_op jit(solution)/shard_map/all_to_all | solution.py:75
  75.8 0.1 copy.85
  75.9 0.2 reshape.38
  76.2 0.3 multiply_reduce_fusion.1
  76.5 0.1 copy.90
  76.6 0.1 slice_add_fusion.18
  76.7 0.1 copy.91
  76.8 0.1 copy.92
  76.9 0.1 copy.86
  77.0 0.2 reshape_reshape.3
  77.2 0.4 fusion.17
  77.7 21.9 %all-to-all-done.1 = f32[4,1,57344]{2,1,0:T(1,128)S(1)} async-done(((f32[4,1,57344]{2,1,0:T(1,128)}), f32[4,1,57344]{2,1,0:T(1,128)S(1)}, u32[]{:S(2)}, u32[]{:S(2)}) %all-to-all-start.1) | async-done | bytes 917536 | tf_op jit(solution)/shard_map/all_to_all | solution.py:75
  99.6 0.5 broadcast.20
  100.1 3.3 %reduce.2 = f32[4,57344]{1,0:T(4,128)S(1)} reduce(f32[4,1,57344]{2,1,0:T(1,128)S(1)} %all-to-all-done.1, f32[]{:T(128)} %broadcast.20), dimensions={1}, to_apply=%all_to_all.15.reduce_sub_computation | reduce | bytes 1835012 | tf_op jit(solution)/shard_map/all_to_all | solution.py:75
  103.4 12.7 %reshape.45 = f32[512,2,16,14]{3,2,1,0:T(8,128)} reshape(f32[4,57344]{1,0:T(4,128)S(1)} %reduce.2) | data formatting | bytes 1835008
  116.1 5.7 %copy.94 = f32[2,16,14,4,128]{4,3,1,2,0:T(4,128)S(1)} copy(f32[2,16,14,4,128]{2,1,0,4,3:T(8,128)} %bitcast.34) | data formatting | bytes 1835008 | tf_op jit(solution)/shard_map/all_to_all | solution.py:75
  121.7 0.2 multiply_reduce_fusion
  122.0 0.5 copy.88
  122.5 1.8 %fusion.13 = f32[512,1792]{1,0:T(8,128)S(1)} fusion(f32[16,8,14,128]{3,2,1,0:T(8,128)S(1)} %bitcast.36, f32[256,64]{1,0:T(8,128)S(1)} %get-tuple-element.19, f32[256,64]{1,0:T(8,128)S(1)} %get-tuple-element.18, f32[256,64]{1,0:T(8,128)S(1)} %get-tuple-element.17), kind=kOutput, calls=%fused_computation.32 | convolution fusion | flops 704839680 | bytes 4784128 | tf_op jit(solution)/shard_map/dot_general | solution.py:49
  124.3 1.5 %fusion = f32[256,1792]{1,0:T(8,128)} fusion(f32[512,1792]{1,0:T(8,128)S(1)} %fusion.13), kind=kLoop, calls=%fused_computation.2 | loop fusion | flops 1376256 | bytes 5505024 | tf_op jit(solution)/shard_map/add | solution.py:50
  125.7 1.8 %copy.89 = f32[256,1792]{0,1:T(8,128)S(1)} copy(f32[256,1792]{1,0:T(8,128)} %fusion) | data formatting | bytes 3670016 | tf_op jit(solution)/shard_map/add | solution.py:50
  127.6 0.2 slice_add_fusion
  127.8 0.1 fusion.23
  127.9 0.9 fusion.12
  128.8 1.1 copy.93
  (19 shorter events, 0.4 us)
Async XLA Ops:
  0.0 13.5 %copy-start = (f32[64]{0:T(128)S(1)}, f32[64]{0:T(128)}, u32[]{:S(2)}) copy-start(f32[64]{0:T(128)} %param.3) | copy-start | bytes 772
  1.5 12.6 %collective-permute-start = (f32[2,16,3,512]{3,1,2,0:T(8,128)S(1)}, f32[2,16,3,512]{3,1,2,0:T(8,128)S(1)}, u32[]{:S(2)}, u32[]{:S(2)}) collective-permute-start(f32[2,16,3,512]{3,1,2,0:T(8,128)S(1)} %copy.95), channel_id=1, source_target_pairs={{0,1},{1,2},{2,3},{3,4},{4,5},{5,6},{6,7},{8,9},{9,10},{10,11},{11... | collective-permute-start | bytes 589832 | tf_op jit(solution)/shard_map/ppermute | solution.py:14
  4.0 17.6 %collective-permute-start.1 = (f32[2,16,3,512]{3,1,2,0:T(8,128)S(1)}, f32[2,16,3,512]{3,1,2,0:T(8,128)S(1)}, u32[]{:S(2)}, u32[]{:S(2)}) collective-permute-start(f32[2,16,3,512]{3,1,2,0:T(8,128)S(1)} %copy.96), channel_id=1, source_target_pairs={{1,0},{2,1},{3,2},{4,3},{5,4},{6,5},{7,6},{9,8},{10,9},{11,10},{12... | collective-permute-start | bytes 589832 | tf_op jit(solution)/shard_map/ppermute | solution.py:15
  41.7 29.0 %all-to-all-start = ((f32[4,32,84]{2,1,0:T(8,128)}), f32[4,32,84]{2,1,0:T(8,128)S(1)}, u32[]{:S(2)}, u32[]{:S(2)}) async-start(f32[4,32,84]{2,1,0:T(8,128)} %pad_maximum_fusion.5), calls=%async_computation | async-start | bytes 131072 | tf_op jit(solution)/shard_map/all_to_all | solution.py:31
  70.7 28.8 %all-to-all-start.1 = ((f32[4,1,57344]{2,1,0:T(1,128)}), f32[4,1,57344]{2,1,0:T(1,128)S(1)}, u32[]{:S(2)}, u32[]{:S(2)}) async-start(f32[4,1,57344]{2,1,0:T(1,128)} %reshape.44), calls=%async_computation.1 | async-start | bytes 1835008 | tf_op jit(solution)/shard_map/all_to_all | solution.py:75
where the time goes:
time: 130 us
  local copies, waits for them, and re-layouts  59.6 us (46%)
  other arithmetic  31.5 us (24%)
  waiting for transfers between devices  21.9 us (17%)
  starting transfers between devices  14.5 us (11%)
  matrix products  2.13 us (2%)
    unnamed x9, local copies, waits for them, and re-layouts  31.4 us
    all_to_all x1, waiting for transfers between devices, body(): lax.all_to_all(tall, 'acq', split_axis=3, concat_axis=1, tiled=True)  21.9 us
    unnamed x1, other arithmetic  13.2 us
    concatenate x1, other arithmetic, with_line_halo(): return jnp.concatenate([before, x, after], axis=2)  10.5 us
    ppermute x1, local copies, waits for them, and re-layouts, with_line_halo(): before = lax.ppermute(x[:, :, length - width:], 'line', up)  7.51 us
    ppermute x1, local copies, waits for them, and re-layouts, with_line_halo(): after = lax.ppermute(x[:, :, :width], 'line', down)  7.5 us
    all_to_all x3, local copies, waits for them, and re-layouts, body(): lax.all_to_all(tall, 'acq', split_axis=3, concat_axis=1, tiled=True)  6.72 us
    all_to_all x1, starting transfers between devices, range_halo(): got = lax.all_to_all(sent, 'acq', split_axis=0, concat_axis=0, tiled=True)  5.69 us
  transfers between devices with their start and end apart: 4, of which 1 were waited for; matrix products, arithmetic and copies ran while one was open for 32% of the time, Pallas kernels for 0%

commit v1 on v0

--- a/solution.py
+++ b/solution.py
@@ -72,7 +72,10 @@
     line_count = slc_stack.shape[2]
     tall = with_line_halo(slc_stack, width)
     edge = range_halo(tall, width)
-    regrouped = lax.all_to_all(tall, "acq", split_axis=3, concat_axis=1, tiled=True)
+    regrouped = jnp.concatenate(
+        lax.all_to_all(jnp.stack(jnp.split(tall, lax.axis_size("acq"), axis=3)), "acq", 0, 0),
+        axis=1,
+    )
     range_count = regrouped.shape[3]
     matrix = steering(wavenumbers, HEIGHTS)
     inner = beamform(regrouped, matrix, HEIGHTS)

time: 130 us -> 59.8 us (0.46)
  the two profiles are of different devices: /device:TPU:0 before, /device:TPU:3 now
where the time goes in v1:
time: 59.8 us; the launch traced here: 59.4 us
  waiting for transfers between devices  29.7 us (50%)
  starting transfers between devices  13.7 us (23%)
  local copies, waits for them, and re-layouts  8.1 us (14%)
  other arithmetic  5.59 us (9%)
  matrix products  2.13 us (4%)
    all_to_all x1, waiting for transfers between devices, body(): lax.all_to_all(jnp.stack(jnp.split(tall, lax.axis_size('acq'), axis=3)),...  21.1 us
    ppermute x1, waiting for transfers between devices, with_line_halo(): after = lax.ppermute(x[:, :, :width], 'line', down)  5.02 us
    all_to_all x1, starting transfers between devices, range_halo(): got = lax.all_to_all(sent, 'acq', split_axis=0, concat_axis=0, tiled=True)  4.59 us
    ppermute x1, starting transfers between devices, with_line_halo(): before = lax.ppermute(x[:, :, length - width:], 'line', up)  3.68 us
    all_to_all x1, waiting for transfers between devices, range_halo(): got = lax.all_to_all(sent, 'acq', split_axis=0, concat_axis=0, tiled=True)  3.56 us
    all_to_all x1, starting transfers between devices, body(): lax.all_to_all(jnp.stack(jnp.split(tall, lax.axis_size('acq'), axis=3)),...  3.5 us
    dot_general x2, matrix products, beamform(): jnp.dot(matrix, flat, precision=lax.Precision.HIGH, preferred_element_typ...  2.13 us
    ppermute x1, starting transfers between devices, with_line_halo(): after = lax.ppermute(x[:, :, :width], 'line', down)  1.92 us
  transfers between devices with their start and end apart: 4, of which 3 were waited for; matrix products, arithmetic and copies ran while one was open for 6% of the time, Pallas kernels for 0%

profile of v1, /device:TPU:3, one launch (start us, length us, event | category | flops | bytes accessed | tf_op | source)
XLA Modules:
  0.0 59.4 jit_solution(10643331105282558041)
XLA Ops:
  0.0 1.4 %fusion.34 = (f32[2,16,3,512]{3,2,1,0:T(4,128)S(1)}, f32[2,16,3,512]{3,2,1,0:T(4,128)S(1)}) fusion(f32[2,16,8,512]{3,2,1,0:T(8,128)} %param.2), kind=kLoop, calls=%fused_computation.94 | loop fusion | bytes 786432 | tf_op jit(solution)/shard_map/slice | solution.py:15
  1.4 0.1 copy.72
  1.5 3.7 %collective-permute-start = (f32[2,16,3,512]{3,1,2,0:T(8,128)S(1)}, f32[2,16,3,512]{3,1,2,0:T(8,128)S(1)}, u32[]{:S(2)}, u32[]{:S(2)}) collective-permute-start(f32[2,16,3,512]{3,1,2,0:T(8,128)S(1)} %copy.72), channel_id=1, source_target_pairs={{0,1},{1,2},{2,3},{3,4},{4,5},{5,6},{6,7},{8,9},{9,10},{10,11},{11... | collective-permute-start | bytes 589832 | tf_op jit(solution)/shard_map/ppermute | solution.py:14
  5.1 0.1 copy.73
  5.2 1.9 %collective-permute-start.1 = (f32[2,16,3,512]{3,1,2,0:T(8,128)S(1)}, f32[2,16,3,512]{3,1,2,0:T(8,128)S(1)}, u32[]{:S(2)}, u32[]{:S(2)}) collective-permute-start(f32[2,16,3,512]{3,1,2,0:T(8,128)S(1)} %copy.73), channel_id=1, source_target_pairs={{1,0},{2,1},{3,2},{4,3},{5,4},{6,5},{7,6},{9,8},{10,9},{11,10},{12... | collective-permute-start | bytes 589832 | tf_op jit(solution)/shard_map/ppermute | solution.py:15
  7.2 0.5 multiply_sine_fusion
  7.8 0.3 constant_dynamic-update-slice_fusion.1
  8.1 5.0 %collective-permute-done.1 = f32[2,16,3,512]{3,1,2,0:T(8,128)S(1)} collective-permute-done((f32[2,16,3,512]{3,1,2,0:T(8,128)S(1)}, f32[2,16,3,512]{3,1,2,0:T(8,128)S(1)}, u32[]{:S(2)}, u32[]{:S(2)}) %collective-permute-start.1) | collective-permute-done | bytes 196640 | tf_op jit(solution)/shard_map/ppermute | solution.py:15
  13.1 0.1 slice_bitcast_fusion.3
  13.2 0.3 fusion.33
  13.5 0.2 copy.64
  13.7 0.1 stack.30
  13.9 0.1 copy.52
  13.9 0.2 copy.65
  14.2 0.1 stack.33
  14.3 0.1 copy.55
  14.4 0.2 pad_maximum_fusion.3
  14.6 0.2 copy.49
  14.8 0.1 stack.31
  14.9 0.1 copy.53
  15.0 0.2 copy.50
  15.3 0.1 stack.32
  15.4 0.1 copy.54
  15.5 0.6 %pad_maximum_fusion.5 = f32[4,32,84]{2,1,0:T(8,128)} fusion(f32[1,32,84]{2,1,0:T(8,128)S(1)} %copy.55, f32[1,32,84]{2,1,0:T(8,128)S(1)} %copy.54, f32[1,32,84]{2,1,0:T(8,128)S(1)} %copy.53, f32[1,32,84]{2,1,0:T(8,128)S(1)} %copy.52), kind=kLoop, calls=%fused_computation.56 | loop fusion | flops 32256 | bytes 86016 | tf_op jit(solution)/shard_map/stack | solution.py:30
  16.1 4.6 %all-to-all-start = ((f32[4,32,84]{2,1,0:T(8,128)}), f32[4,32,84]{2,1,0:T(8,128)S(1)}, u32[]{:S(2)}, u32[]{:S(2)}) async-start(f32[4,32,84]{2,1,0:T(8,128)} %pad_maximum_fusion.5), calls=%async_computation | async-start | bytes 131072 | tf_op jit(solution)/shard_map/all_to_all | solution.py:31
  20.7 1.0 %pad_maximum_fusion.2 = f32[4,2,16,14,128]{4,2,3,1,0:T(8,128)} fusion(f32[1,2,16,14,128]{4,2,3,1,0:T(8,128)S(1)} %get-tuple-element.6, f32[1,2,16,14,128]{4,2,3,1,0:T(8,128)S(1)} %get-tuple-element.7, f32[1,2,16,14,128]{4,2,3,1,0:T(8,128)S(1)} %get-tuple-element.8, f32[1,2,16,14,128]{4,2,3,1,0:T(8,128)S(1)} %get-tuple-element.5), kind=kLoop, calls=%fused_computation.34 | loop fusion | flops 688128 | bytes 1835008 | tf_op jit(solution)/shard_map/stack | solution.py:76
  21.7 3.6 %all-to-all-done = f32[4,32,84]{2,1,0:T(8,128)S(1)} async-done(((f32[4,32,84]{2,1,0:T(8,128)}), f32[4,32,84]{2,1,0:T(8,128)S(1)}, u32[]{:S(2)}, u32[]{:S(2)}) %all-to-all-start) | async-done | bytes 43040 | tf_op jit(solution)/shard_map/all_to_all | solution.py:31
  25.3 3.5 %all-to-all-start.1 = ((f32[4,2,16,14,128]{4,2,3,1,0:T(8,128)}), f32[4,2,16,14,128]{4,2,3,1,0:T(8,128)S(1)}, u32[]{:S(2)}, u32[]{:S(2)}) async-start(f32[4,2,16,14,128]{4,2,3,1,0:T(8,128)} %pad_maximum_fusion.2), calls=%async_computation.1 | async-start | bytes 1835008 | tf_op jit(solution)/shard_map/all_to_all | solution.py:76
  28.8 0.1 copy.56
  28.9 0.2 reshape.37
  29.2 0.3 multiply_reduce_fusion.1
  29.5 0.1 copy.60
  29.6 0.1 slice_add_fusion.18
  29.7 0.1 copy.61
  29.8 0.1 copy.62
  29.9 0.1 copy.57
  30.0 0.2 reshape_reshape.6
  30.2 0.4 fusion.17
  30.7 21.1 %all-to-all-done.1 = f32[4,2,16,14,128]{4,2,3,1,0:T(8,128)S(1)} async-done(((f32[4,2,16,14,128]{4,2,3,1,0:T(8,128)}), f32[4,2,16,14,128]{4,2,3,1,0:T(8,128)S(1)}, u32[]{:S(2)}, u32[]{:S(2)}) %all-to-all-start.1) | async-done | bytes 917536 | tf_op jit(solution)/shard_map/all_to_all | solution.py:76
  51.7 0.1 multiply_reduce_fusion
  51.8 0.3 copy.58
  52.1 1.8 %fusion.13 = f32[512,1792]{1,0:T(8,128)S(1)} fusion(f32[16,8,14,128]{3,2,1,0:T(8,128)S(1)} %bitcast.39, f32[256,64]{1,0:T(8,128)S(1)} %get-tuple-element.23, f32[256,64]{1,0:T(8,128)S(1)} %get-tuple-element.22, f32[256,64]{1,0:T(8,128)S(1)} %get-tuple-element.21), kind=kOutput, calls=%fused_computation.31 | convolution fusion | flops 704839680 | bytes 4784128 | tf_op jit(solution)/shard_map/dot_general | solution.py:49
  53.9 1.4 %fusion = f32[256,1792]{1,0:T(8,128)} fusion(f32[512,1792]{1,0:T(8,128)S(1)} %fusion.13), kind=kLoop, calls=%fused_computation.1 | loop fusion | flops 1376256 | bytes 5505024 | tf_op jit(solution)/shard_map/add | solution.py:50
  55.3 1.8 %copy.59 = f32[256,1792]{0,1:T(8,128)S(1)} copy(f32[256,1792]{1,0:T(8,128)} %fusion) | data formatting | bytes 3670016 | tf_op jit(solution)/shard_map/add | solution.py:50
  57.1 0.2 slice_add_fusion
  57.4 0.1 fusion.23
  57.5 0.9 %fusion.12 = bf16[256,8,128]{0,2,1:T(8,128)(2,1)S(1)} fusion(f32[256,8,3]{0,2,1:T(4,128)S(1)} %get-tuple-element.18, f32[256,8,128]{0,2,1:T(8,128)S(1)} %slice_add_fusion, f32[256,8,3]{0,2,1:T(4,128)S(1)} %get-tuple-element.17, f32[8,128]{1,0:T(8,128)S(1)} %fusion.23), kind=kLoop, calls=%fused_computation.30 | loop fusion | flops 3670016 | bytes 1626112 | tf_op jit(solution)/shard_map/convert_element_type | solution.py:88
  58.3 1.1 %copy.63 = bf16[256,8,128]{2,1,0:T(8,128)(2,1)} copy(bf16[256,8,128]{0,2,1:T(8,128)(2,1)S(1)} %fusion.12) | data formatting | bytes 1048576 | tf_op jit(solution)/shard_map/convert_element_type | solution.py:88
  (16 shorter events, 0.2 us)
Async XLA Ops:
  0.0 7.8 %copy-start = (f32[2,16,8,512]{3,2,1,0:T(8,128)S(1)}, f32[2,16,8,512]{3,2,1,0:T(8,128)}, u32[]{:S(2)}) copy-start(f32[2,16,8,512]{3,2,1,0:T(8,128)} %param.2) | copy-start | bytes 1572868
  0.0 7.2 %copy-start.1 = (f32[64]{0:T(128)S(1)}, f32[64]{0:T(128)}, u32[]{:S(2)}) copy-start(f32[64]{0:T(128)} %param.3) | copy-start | bytes 772
  1.5 6.3 %collective-permute-start = (f32[2,16,3,512]{3,1,2,0:T(8,128)S(1)}, f32[2,16,3,512]{3,1,2,0:T(8,128)S(1)}, u32[]{:S(2)}, u32[]{:S(2)}) collective-permute-start(f32[2,16,3,512]{3,1,2,0:T(8,128)S(1)} %copy.72), channel_id=1, source_target_pairs={{0,1},{1,2},{2,3},{3,4},{4,5},{5,6},{6,7},{8,9},{9,10},{10,11},{11... | collective-permute-start | bytes 589832 | tf_op jit(solution)/shard_map/ppermute | solution.py:14
  5.2 7.9 %collective-permute-start.1 = (f32[2,16,3,512]{3,1,2,0:T(8,128)S(1)}, f32[2,16,3,512]{3,1,2,0:T(8,128)S(1)}, u32[]{:S(2)}, u32[]{:S(2)}) collective-permute-start(f32[2,16,3,512]{3,1,2,0:T(8,128)S(1)} %copy.73), channel_id=1, source_target_pairs={{1,0},{2,1},{3,2},{4,3},{5,4},{6,5},{7,6},{9,8},{10,9},{11,10},{12... | collective-permute-start | bytes 589832 | tf_op jit(solution)/shard_map/ppermute | solution.py:15
  16.1 9.2 %all-to-all-start = ((f32[4,32,84]{2,1,0:T(8,128)}), f32[4,32,84]{2,1,0:T(8,128)S(1)}, u32[]{:S(2)}, u32[]{:S(2)}) async-start(f32[4,32,84]{2,1,0:T(8,128)} %pad_maximum_fusion.5), calls=%async_computation | async-start | bytes 131072 | tf_op jit(solution)/shard_map/all_to_all | solution.py:31
  25.3 26.4 %all-to-all-start.1 = ((f32[4,2,16,14,128]{4,2,3,1,0:T(8,128)}), f32[4,2,16,14,128]{4,2,3,1,0:T(8,128)S(1)}, u32[]{:S(2)}, u32[]{:S(2)}) async-start(f32[4,2,16,14,128]{4,2,3,1,0:T(8,128)} %pad_maximum_fusion.2), calls=%async_computation.1 | async-start | bytes 1835008 | tf_op jit(solution)/shard_map/all_to_all | solution.py:76
